TPU v7x, 256 devices: a whole 4x4x8 slice. The times are simulated.
256 devices in a mesh: ep: 64 (over z, y, core), rep: 4 (over x).
Axes of the slice: x: 4, y: 4, z: 8, core: 2. Of those that a mesh axis runs over, the one named last changes fastest.
Arguments:
- residual: bfloat16 [4096, 2048], P('ep'), may hold values from -6 to 6
- query_latent: bfloat16 [4096, 8192], P(('ep', 'rep')), may hold values from -32.5 to 32.5
- query_rope: bfloat16 [4096, 1024], P(('ep', 'rep')), may hold values from -4 to 4
- cache_latent: bfloat16 [8192, 32, 512], P(('ep', 'rep')), may hold values from -4.6 to 4.6
- cache_rope: bfloat16 [8192, 2048], P(('ep', 'rep')), may hold values from -4 to 4
- page_table: int32 [4096, 9], P(('ep', 'rep')), may hold values from 0 to 31, as said below
- lengths: int32 [4096], P(('ep', 'rep')), may hold values from 257 to 288, as said below
- value_up: bfloat16 [16, 512, 128], P('rep'), may hold values from -0.25 to 0.25
- out_proj: bfloat16 [2048, 2048], P('rep'), may hold values from -0.125 to 0.125
- routes: int32 [4096, 6], P('ep'), may hold values from 0 to 63, all different within a row; in each aligned block of 64 rows (0 to 63, 64 to 127, ...) at most 12 rows name the same one
- route_weight: float32 [4096, 6], P('ep'), may hold values from 0.05 to 0.6
- placement: int32 [64], replicated, may hold values from 0 to 63, each once
- expert_gate: bfloat16 [64, 2048, 1408], P('ep', None, 'rep'), may hold values from -0.125 to 0.125
- expert_up: bfloat16 [64, 2048, 1408], P('ep', None, 'rep'), may hold values from -0.125 to 0.125
- expert_down: bfloat16 [64, 1408, 2048], P('ep', 'rep'), may hold values from -0.15625 to 0.15625
- shared_gate: bfloat16 [2048, 1408], P(None, 'rep'), may hold values from -0.125 to 0.125
- shared_up: bfloat16 [2048, 1408], P(None, 'rep'), may hold values from -0.125 to 0.125
- shared_down: bfloat16 [1408, 2048], P('rep'), may hold values from -0.15625 to 0.15625
- norm_gain: float32 [2048], replicated, may hold values from 0.5 to 1.5
Outputs:
- normed: bfloat16 [4096, 2048], P(('ep', 'rep'))
Inputs may be any that keep to these rules, and one draw needn't show every extreme that they name: `page_table`: entries number the 32 pages of the row's own device. A device's rows come in consecutive groups of 8 that share their first 8 entries; all other entries of a device are distinct. `lengths`: every row's context covers its shared prompt; the last row of every device has the greatest length. `routes`: within the 64 rows of one index of ep, no expert is named by more than 12 rows, a bound that some block reaches. `placement`: each slot holds exactly one expert.
All inputs are finite; a program needn't handle non-finite values.
Results may differ from a plain program's by a relative error of at most 0.014.
Values may be sent and summed in bfloat16 or wider, within the bound.
A program may use at most 128 MiB of HBM per device.

v0:
```python
import math
import jax
import jax.numpy as jnp
from jax import lax
from jax.sharding import PartitionSpec as P

ROPE = 64
VHEAD = 128
EPSILON = 1e-06


def attend_rows(query_latent, query_rope, cache_latent, cache_rope, page_table, lengths):
    row_count = page_table.shape[0]
    page_len = cache_latent.shape[1]
    latent_width = cache_latent.shape[2]
    rope_width = cache_rope.shape[1] // page_len
    head_count = query_rope.shape[1] // rope_width
    key_span = page_table.shape[1] * page_len
    keys_lat = cache_latent[page_table].reshape(row_count, key_span, latent_width)
    keys_rope = cache_rope[page_table].reshape(row_count, key_span, rope_width)
    query_lat = query_latent.reshape(row_count, head_count, latent_width)
    query_rot = query_rope.reshape(row_count, head_count, rope_width)
    score_scale = 1.0 / math.sqrt(VHEAD + ROPE)
    scores = (
        jnp.einsum("thr,tlr->thl", query_lat, keys_lat, preferred_element_type=jnp.float32)
        + jnp.einsum("thr,tlr->thl", query_rot, keys_rope, preferred_element_type=jnp.float32)
    ) * score_scale
    live_mask = (jnp.arange(key_span, dtype=jnp.int32)[None, :] < lengths[:, None])[:, None, :]
    masked = jnp.where(live_mask, scores, -jnp.inf)
    row_peak = jnp.max(masked, axis=2, keepdims=True)
    expons = jnp.where(live_mask, jnp.exp(scores - row_peak), 0.0)
    probs = (expons / jnp.sum(expons, axis=2, keepdims=True)).astype(jnp.bfloat16)
    latent_out = jnp.einsum("thl,tlr->thr", probs, keys_lat, preferred_element_type=jnp.float32)
    return latent_out.astype(jnp.bfloat16)


def per_device(
    residual,
    query_latent,
    query_rope,
    cache_latent,
    cache_rope,
    page_table,
    lengths,
    value_up,
    out_proj,
    routes,
    route_weight,
    placement,
    expert_gate,
    expert_up,
    expert_down,
    shared_gate,
    shared_up,
    shared_down,
    norm_gain,
):
    replicas = lax.axis_size("rep")
    expert_groups = lax.axis_size("ep")
    latent_out = attend_rows(
        query_latent, query_rope, cache_latent, cache_rope, page_table, lengths
    )
    own_count = latent_out.shape[0]
    swapped = lax.all_to_all(latent_out, "rep", split_axis=1, concat_axis=0, tiled=True)
    group_rows = swapped.shape[0]
    head_out = jnp.einsum(
        "thr,hrv->thv", swapped, value_up, preferred_element_type=jnp.float32
    ).astype(jnp.bfloat16)
    attn_terms = jnp.dot(
        head_out.reshape(group_rows, -1), out_proj, preferred_element_type=jnp.float32
    )
    attended = lax.psum(attn_terms.astype(jnp.bfloat16), "rep")
    hidden = (residual.astype(jnp.float32) + attended.astype(jnp.float32)).astype(jnp.bfloat16)
    model_width = hidden.shape[1]
    shared_act = (
        jax.nn.silu(jnp.dot(hidden, shared_gate, preferred_element_type=jnp.float32))
        * jnp.dot(hidden, shared_up, preferred_element_type=jnp.float32)
    ).astype(jnp.bfloat16)
    shared_terms = jnp.dot(shared_act, shared_down, preferred_element_type=jnp.float32)
    experts = placement.shape[0]
    route_count = routes.shape[1]
    per_group = experts // expert_groups
    capacity = max(
        replicas, min(group_rows, 2 * group_rows * route_count // experts // replicas * replicas)
    )
    expert_ids = jnp.arange(experts, dtype=jnp.int32)
    slot_index = jnp.sum(jnp.where(routes[:, :, None] == expert_ids, placement, 0), axis=2).reshape(
        -1
    )
    one_hot = (slot_index[:, None] == expert_ids[None, :]).astype(jnp.int32)
    earlier = jnp.cumsum(one_hot, axis=0) - one_hot
    position = jnp.sum(earlier * one_hot, axis=1)
    assignments = slot_index.shape[0]
    source_row = (
        jnp.full((experts * capacity,), group_rows, jnp.int32)
        .at[slot_index * capacity + position]
        .set(jnp.arange(assignments, dtype=jnp.int32) // route_count)
    )
    padded = jnp.concatenate([hidden, jnp.zeros((1, model_width), jnp.bfloat16)], axis=0)
    outgoing = padded[source_row].reshape(expert_groups, per_group * capacity, model_width)
    incoming = lax.all_to_all(outgoing, "ep", split_axis=0, concat_axis=0, tiled=True).reshape(
        expert_groups, per_group, capacity, model_width
    )
    gate_values = jnp.einsum(
        "secd,edf->secf", incoming, expert_gate, preferred_element_type=jnp.float32
    )
    up_values = jnp.einsum(
        "secd,edf->secf", incoming, expert_up, preferred_element_type=jnp.float32
    )
    activated = (jax.nn.silu(gate_values) * up_values).astype(jnp.bfloat16)
    expert_terms = jnp.einsum(
        "secf,efd->secd", activated, expert_down, preferred_element_type=jnp.float32
    )
    outbound = expert_terms.astype(jnp.bfloat16).reshape(
        expert_groups, per_group * capacity, model_width
    )
    returned = lax.all_to_all(outbound, "ep", split_axis=0, concat_axis=0, tiled=True)
    picked = returned.reshape(experts * capacity, model_width)[slot_index * capacity + position]
    weight_used = route_weight.reshape(-1)
    routed = jnp.sum(
        (picked.astype(jnp.float32) * weight_used[:, None]).reshape(
            group_rows, route_count, model_width
        ),
        axis=1,
    )
    row_sums = lax.psum_scatter(
        (routed + shared_terms).astype(jnp.bfloat16), "rep", scatter_dimension=0, tiled=True
    ).astype(jnp.float32)
    own_hidden = lax.dynamic_slice_in_dim(hidden, lax.axis_index("rep") * own_count, own_count, 0)
    mixed = row_sums + own_hidden.astype(jnp.float32)
    inverse = lax.rsqrt(jnp.mean(mixed * mixed, axis=1, keepdims=True) + EPSILON)
    return (mixed * inverse * norm_gain).astype(jnp.bfloat16)


def solution(mesh):
    in_specs = (
        P("ep", None),
        P(("ep", "rep"), None),
        P(("ep", "rep"), None),
        P(("ep", "rep"), None, None),
        P(("ep", "rep"), None),
        P(("ep", "rep"), None),
        P(("ep", "rep")),
        P("rep", None, None),
        P("rep", None),
        P("ep", None),
        P("ep", None),
        P(),
        P("ep", None, "rep"),
        P("ep", None, "rep"),
        P("ep", "rep", None),
        P(None, "rep"),
        P(None, "rep"),
        P("rep", None),
        P(),
    )
    out_specs = P(("ep", "rep"), None)
    return jax.shard_map(
        per_device, mesh=mesh, in_specs=in_specs, out_specs=out_specs, check_vma=False
    )
```

profile of v0, /device:TPU:8, one launch (start us, length us, event | category | flops | bytes accessed | tf_op | source)
XLA Modules:
  0.0 386.6 jit_solution(4769839513103228752)
XLA Ops:
  7.5 1.0 copy.57
  8.5 8.8 %gather_fusion = bf16[144,32,512]{2,1,0:T(8,128)(2,1)} fusion(bf16[32,32,512]{2,1,0:T(8,128)(2,1)} %param.22, s32[1024]{0:T(1024)S(1)} %pad_clamp_fusion.2), kind=kCustom, calls=%fused_computation | custom fusion | bytes 9437760 | tf_op jit(solution)/shard_map/gather | solution.py:19
  17.3 1.8 gather_fusion.1
  19.2 2.2 reshape.130
  21.4 1.5 reshape.131
  23.0 3.7 fusion.79
  28.2 3.5 convolution_convert_fusion.2
  32.6 4.3 %all-to-all-start = ((bf16[16,16,512]{2,0,1:T(8,128)(2,1)}), bf16[16,16,512]{2,0,1:T(8,128)(2,1)S(1)}, u32[]{:S(2)}, u32[]{:S(2)}) async-start(bf16[16,16,512]{2,0,1:T(8,128)(2,1)} %copy.43), calls=%async_computation | async-start | bytes 524288 | tf_op jit(solution)/shard_map/all_to_all | solution.py:64
  37.6 0.9 reduce-window.6
  39.1 2.9 scatter_custom_fusion
  42.1 1.5 all-to-all-done
  43.8 1.2 convolution_convert_fusion.1
  45.1 48.8 %all-reduce.3.cloned.1.call-done = bf16[64,2048]{1,0:T(8,128)(2,1)} async-done(((bf16[64,2048]{1,0:T(8,128)(2,1)}), bf16[64,2048]{1,0:T(8,128)(2,1)}) %all-reduce.3.cloned.1.call-update) | async-done | bytes 262160 | tf_op jit(solution)/shard_map/psum | solution.py:72
  93.9 1.0 add_convert_fusion
  94.9 4.3 %gather_fusion.2 = bf16[768,2048]{1,0:T(8,128)(2,1)} fusion(bf16[65,2048]{1,0:T(8,128)(2,1)S(1)} %concatenate.3, s32[1024]{0:T(1024)S(1)} %pad_clamp_fusion.1), kind=kCustom, calls=%fused_computation.2 | custom fusion | bytes 6294528 | tf_op jit(solution)/shard_map/gather | solution.py:100
  99.2 6.1 %reshape.134 = bf16[64,12,2048]{2,1,0:T(8,128)(2,1)} reshape(bf16[768,2048]{1,0:T(8,128)(2,1)} %gather_fusion.2) | data formatting | bytes 6291456 | tf_op jit(solution)/shard_map/reshape | solution.py:100
  105.3 106.9 %all_to_all.28 = bf16[64,12,2048]{2,1,0:T(8,128)(2,1)S(1)} all-to-all(bf16[64,12,2048]{2,1,0:T(8,128)(2,1)} %reshape.134), channel_id=1, replica_groups=mesh['ep'=64,'rep'=4] {'ep'}, dimensions={0} | all-to-all | bytes 6291456 | tf_op jit(solution)/shard_map/all_to_all | solution.py:101
  212.1 2.0 copy-done.2
  214.2 3.1 fusion.9
  217.2 8.8 %convolution_convert_fusion = bf16[64,12,2048]{2,0,1:T(8,128)(2,1)} fusion(bf16[1,352,2048]{2,1,0:T(8,128)(2,1)} %param.33, bf16[1,2048,352]{1,2,0:T(8,128)(2,1)} %param.32, bf16[64,12,2048]{2,1,0:T(8,128)(2,1)} %copy-done.2, f32[64,1,12,352]{3,0,2,1:T(8,128)} %fusion.9), kind=kOutput, calls=%fused_computation.7 | convolution fusion | flops 2217787392 | bytes 10256384 | tf_op jit(solution)/shard_map/secf,efd->secd/dot_general | solution.py:111
  226.0 5.7 %copy.52 = bf16[64,12,2048]{2,1,0:T(8,128)(2,1)} copy(bf16[64,12,2048]{2,0,1:T(8,128)(2,1)} %convolution_convert_fusion) | data formatting | bytes 6291456 | tf_op jit(solution)/shard_map/convert_element_type | solution.py:114
  231.7 5.8 %all-to-all-start.2 = ((bf16[64,12,2048]{2,1,0:T(8,128)(2,1)}), bf16[64,12,2048]{2,1,0:T(8,128)(2,1)}, u32[]{:S(2)}, u32[]{:S(2)}) async-start(bf16[64,12,2048]{2,1,0:T(8,128)(2,1)} %copy.52), calls=%async_computation.2 | async-start | bytes 8388608 | tf_op jit(solution)/shard_map/all_to_all | solution.py:117
  237.8 1.9 fusion.80
  239.7 93.9 %all-to-all-done.2 = bf16[64,12,2048]{2,1,0:T(8,128)(2,1)} async-done(((bf16[64,12,2048]{2,1,0:T(8,128)(2,1)}), bf16[64,12,2048]{2,1,0:T(8,128)(2,1)}, u32[]{:S(2)}, u32[]{:S(2)}) %all-to-all-start.2) | async-done | bytes 3145760 | tf_op jit(solution)/shard_map/all_to_all | solution.py:117
  333.6 6.2 %reshape.139 = bf16[768,2048]{1,0:T(8,128)(2,1)} reshape(bf16[64,12,2048]{2,1,0:T(8,128)(2,1)} %all-to-all-done.2) | data formatting | bytes 6291456 | tf_op jit(solution)/shard_map/reshape | solution.py:118
  339.8 7.4 %gather_fusion.3 = bf16[384,2048]{1,0:T(8,128)(2,1)} fusion(bf16[768,2048]{1,0:T(8,128)(2,1)} %reshape.139, s32[1024]{0:T(1024)S(1)} %pad_clamp_fusion), kind=kCustom, calls=%fused_computation.3 | custom fusion | bytes 3147264 | tf_op jit(solution)/shard_map/gather | solution.py:118
  347.1 3.9 %reshape.140 = f32[64,6,2048]{2,1,0:T(8,128)} reshape(bf16[384,2048]{1,0:T(8,128)(2,1)} %gather_fusion.3) | data formatting | bytes 4718592 | tf_op jit(solution)/shard_map/convert_element_type | solution.py:121
  351.1 3.7 multiply_reduce_fusion
  354.8 3.7 fusion.1
  358.5 18.6 %reduce-scatter.2.cloned.1.call-done = bf16[16,2048]{1,0:T(8,128)(2,1)} async-done(((bf16[64,2048]{1,0:T(8,128)(2,1)}), bf16[16,2048]{1,0:T(8,128)(2,1)}) %reduce-scatter.2.cloned.1.call-update) | async-done | bytes 65552 | tf_op jit(solution)/shard_map/reduce_scatter | solution.py:126
  377.2 1.0 multiply_reduce_fusion.1
  378.2 1.6 multiply_convert_fusion
  (57 shorter events, 5.4 us)
Async XLA Ops:
  6.5 37.3 %copy-start = (bf16[512,2048]{1,0:T(8,128)(2,1)S(1)}, bf16[512,2048]{1,0:T(8,128)(2,1)}, u32[]{:S(2)}) copy-start(bf16[512,2048]{1,0:T(8,128)(2,1)} %param.27) | copy-start | bytes 6291460
  8.5 8.8 %copy-start.1 = (bf16[32,2048]{1,0:T(8,128)(2,1)S(1)}, bf16[32,2048]{1,0:T(8,128)(2,1)}, u32[]{:S(2)}) copy-start(bf16[32,2048]{1,0:T(8,128)(2,1)} %param.23) | copy-start | bytes 393220
  19.2 3.7 copy-start.11
  23.0 3.7 copy-start.6
  27.1 0.8 copy-start.3
  28.1 8.7 %copy-start.9 = (s32[64,6]{0,1:T(8,128)S(1)}, s32[64,6]{0,1:T(8,128)}, u32[]{:S(2)}) copy-start(s32[64,6]{0,1:T(8,128)} %param.28) | copy-start | bytes 4612
  28.1 8.7 %copy-start.10 = (s32[64]{0:T(128)S(1)}, s32[64]{0:T(128)}, u32[]{:S(2)}) copy-start(s32[64]{0:T(128)} %param.30) | copy-start | bytes 772
  31.7 11.9 %copy-start.4 = (bf16[4,512,128]{2,1,0:T(8,128)(2,1)S(1)}, bf16[4,512,128]{2,1,0:T(8,128)(2,1)}, u32[]{:S(2)}) copy-start(bf16[4,512,128]{2,1,0:T(8,128)(2,1)} %param.26) | copy-start | bytes 1572868
  32.6 11.0 %all-to-all-start = ((bf16[16,16,512]{2,0,1:T(8,128)(2,1)}), bf16[16,16,512]{2,0,1:T(8,128)(2,1)S(1)}, u32[]{:S(2)}, u32[]{:S(2)}) async-start(bf16[16,16,512]{2,0,1:T(8,128)(2,1)} %copy.43), calls=%async_computation | async-start | bytes 524288 | tf_op jit(solution)/shard_map/all_to_all | solution.py:64
  36.9 57.0 %all-reduce.3.cloned.1.call-start = ((), (), s32[]{:S(2)}) async-start(), calls=%async_computation.4 | async-start | bytes 524288 | tf_op jit(solution)/shard_map/psum | solution.py:72
  43.6 50.3 %copy-start.5 = (bf16[64,2048]{1,0:T(8,128)(2,1)S(1)}, bf16[64,2048]{1,0:T(8,128)(2,1)}, u32[]{:S(2)}) copy-start(bf16[64,2048]{1,0:T(8,128)(2,1)} %param.19) | copy-start | bytes 786436
  105.3 108.9 %copy-start.12 = (bf16[1,2048,352]{1,2,0:T(8,128)(2,1)S(1)}, bf16[1,2048,352]{1,2,0:T(8,128)(2,1)}, u32[]{:S(2)}) copy-start(bf16[1,2048,352]{1,2,0:T(8,128)(2,1)} %param.31) | copy-start | bytes 4325380
  212.1 2.0 copy-start.2
  231.7 6.0 %copy-start.8 = (f32[64,6]{0,1:T(8,128)S(1)}, f32[64,6]{0,1:T(8,128)}, u32[]{:S(2)}) copy-start(f32[64,6]{0,1:T(8,128)} %param.29) | copy-start | bytes 4612
  231.7 101.9 %all-to-all-start.2 = ((bf16[64,12,2048]{2,1,0:T(8,128)(2,1)}), bf16[64,12,2048]{2,1,0:T(8,128)(2,1)}, u32[]{:S(2)}, u32[]{:S(2)}) async-start(bf16[64,12,2048]{2,1,0:T(8,128)(2,1)} %copy.52), calls=%async_computation.2 | async-start | bytes 8388608 | tf_op jit(solution)/shard_map/all_to_all | solution.py:117
  237.4 139.7 %reduce-scatter.2.cloned.1.call-start = ((), (), s32[]{:S(2)}) async-start(), calls=%async_computation.5 | async-start | bytes 327680 | tf_op jit(solution)/shard_map/reduce_scatter | solution.py:126
  354.8 23.3 %copy-start.7 = (f32[2048]{0:T(1024)S(1)}, f32[2048]{0:T(1024)}, u32[]{:S(2)}) copy-start(f32[2048]{0:T(1024)} %param.37) | copy-start | bytes 24580
Sparse Core Ops, SparseCore 0:
  45.2 48.6 all-reduce.2
  358.6 18.4 reduce-scatter.1
where the time goes:
time: 388 us; the launch traced here: 387 us
  waiting for transfers between devices  163 us (42%)
  blocking collectives  107 us (28%)
  local copies, waits for them, and re-layouts  56.5 us (15%)
  matrix products  26.6 us (7%)
  between operations  13.7 us (4%)
  starting transfers between devices  10.3 us (3%)
  other arithmetic  9.84 us (3%)
    all_to_all x1, blocking collectives, per_device(): lax.all_to_all(outgoing, 'ep', split_axis=0, concat_axis=0, tiled=True)  107 us
    all_to_all x1, waiting for transfers between devices, per_device(): lax.all_to_all(outbound, 'ep', split_axis=0, concat_axis=0, tiled=True)  93.9 us
    psum x1, waiting for transfers between devices, per_device(): attended = lax.psum(attn_terms.astype(jnp.bfloat16), 'rep')  48.8 us
    reduce_scatter x1, waiting for transfers between devices, per_device(): lax.psum_scatter((routed + shared_terms).astype(jnp.bfloat16), 'rep', sca...  18.6 us
    dot_general x1, matrix products, per_device(): jnp.einsum('secf,efd->secd', activated, expert_down, preferred_element_ty...  8.8 us
    gather x1, local copies, waits for them, and re-layouts, attend_rows(): cache_latent[page_table].reshape(row_count, key_span, latent_width)  8.79 us
  transfers between devices with their start and end apart: 4, of which 4 were waited for; matrix products, arithmetic and copies ran while one was open for 2% of the time, Pallas kernels for 0%

commit v1 on v0

--- a/solution.py
+++ b/solution.py
@@ -69,7 +69,7 @@
     attn_terms = jnp.dot(
         head_out.reshape(group_rows, -1), out_proj, preferred_element_type=jnp.float32
     )
-    attended = lax.psum(attn_terms.astype(jnp.bfloat16), "rep")
+    attended = jnp.sum(lax.all_gather(attn_terms.astype(jnp.bfloat16), "rep"), axis=0)
     hidden = (residual.astype(jnp.float32) + attended.astype(jnp.float32)).astype(jnp.bfloat16)
     model_width = hidden.shape[1]
     shared_act = (

time: 388 us -> 366 us (0.943)
  waiting for transfers between devices: 163 us -> 135 us
  blocking collectives: 107 us -> 118 us
  starting transfers between devices: 10.3 us -> 6.02 us
    psum x1 -> x0, waiting for transfers between devices: 48.8 us -> none  [per_device(): attended = lax.psum(attn_terms.astype(jnp.bfloat16), 'rep')]
    all_gather x0 -> x1, waiting for transfers between devices: none -> 22.4 us  [per_device(): lax.all_gather(attn_terms.astype(jnp.bfloat16), 'rep')]
    all_to_all x0 -> x1, blocking collectives: none -> 10.8 us  [per_device(): lax.all_to_all(latent_out, 'rep', split_axis=1, concat_axis=0, tiled=True)]
    all_to_all x1 -> x0, starting transfers between devices: 4.29 us -> none  [per_device(): lax.all_to_all(latent_out, 'rep', split_axis=1, concat_axis=0, tiled=True)]
  transfers between devices with their start and end apart: 4 -> 3, of which waited for: 4 -> 3; matrix products, arithmetic and copies ran while one was open for 2% -> 2% of each run, Pallas kernels for 0% -> 0%
where the time goes in v1:
time: 366 us; the launch traced here: 365 us
  waiting for transfers between devices  135 us (37%)
  blocking collectives  118 us (32%)
  local copies, waits for them, and re-layouts  55.8 us (15%)
  matrix products  26.6 us (7%)
  between operations  13.7 us (4%)
  other arithmetic  10.3 us (3%)
  starting transfers between devices  6.02 us (2%)
    all_to_all x1, blocking collectives, per_device(): lax.all_to_all(outgoing, 'ep', split_axis=0, concat_axis=0, tiled=True)  107 us
    all_to_all x1, waiting for transfers between devices, per_device(): lax.all_to_all(outbound, 'ep', split_axis=0, concat_axis=0, tiled=True)  93.9 us
    all_gather x1, waiting for transfers between devices, per_device(): lax.all_gather(attn_terms.astype(jnp.bfloat16), 'rep')  22.4 us
    reduce_scatter x1, waiting for transfers between devices, per_device(): lax.psum_scatter((routed + shared_terms).astype(jnp.bfloat16), 'rep', sca...  18.5 us
    all_to_all x1, blocking collectives, per_device(): lax.all_to_all(latent_out, 'rep', split_axis=1, concat_axis=0, tiled=True)  10.8 us
    dot_general x1, matrix products, per_device(): jnp.einsum('secf,efd->secd', activated, expert_down, preferred_element_ty...  8.8 us
    gather x1, local copies, waits for them, and re-layouts, attend_rows(): cache_latent[page_table].reshape(row_count, key_span, latent_width)  8.79 us
    gather x1, local copies, waits for them, and re-layouts, per_device(): returned.reshape(experts * capacity, model_width)  7.37 us
  transfers between devices with their start and end apart: 3, of which 3 were waited for; matrix products, arithmetic and copies ran while one was open for 2% of the time, Pallas kernels for 0%

profile of v1, /device:TPU:8, one launch (start us, length us, event | category | flops | bytes accessed | tf_op | source)
XLA Modules:
  0.0 364.8 jit_solution(3243508446039053008)
XLA Ops:
  6.5 0.8 compare_select_fusion
  7.5 1.0 copy.57
  8.5 8.8 %gather_fusion = bf16[144,32,512]{2,1,0:T(8,128)(2,1)} fusion(bf16[32,32,512]{2,1,0:T(8,128)(2,1)} %param.22, s32[1024]{0:T(1024)S(1)} %pad_clamp_fusion.2), kind=kCustom, calls=%fused_computation | custom fusion | bytes 9437760 | tf_op jit(solution)/shard_map/gather | solution.py:19
  17.3 1.8 gather_fusion.1
  19.2 2.2 reshape.130
  21.4 1.5 reshape.131
  23.0 3.7 %fusion.79 = f32[16,288,16]{1,2,0:T(8,128)S(1)} fusion(bf16[16,288,512]{2,1,0:T(8,128)(2,1)} %bitcast.101, bf16[16,16,512]{2,1,0:T(8,128)(2,1)S(1)} %bitcast.106), kind=kOutput, calls=%fused_computation.89 | convolution fusion | flops 75497472 | bytes 5275648 | tf_op jit(solution)/shard_map/thr,tlr->thl/dot_general | solution.py:25
  28.1 3.5 convolution_convert_fusion.2
  31.9 10.8 %all_to_all.28 = bf16[16,16,512]{2,0,1:T(8,128)(2,1)S(1)} all-to-all(bf16[16,16,512]{2,0,1:T(8,128)(2,1)S(1)} %copy.43), channel_id=1, replica_groups=mesh['ep'=64,'rep'=4] {'rep'}, dimensions={1} | all-to-all | bytes 524288 | tf_op jit(solution)/shard_map/all_to_all | solution.py:64
  42.9 1.2 convolution_convert_fusion.1
  44.8 0.9 reduce-window.6
  46.4 2.9 scatter_custom_fusion
  49.4 22.4 %all-gather.3.cloned.1.call-done = bf16[256,2048]{1,0:T(8,128)(2,1)} async-done(((bf16[64,2048]{1,0:T(8,128)(2,1)}), bf16[256,2048]{1,0:T(8,128)(2,1)}) %all-gather.3.cloned.1.call-update) | async-done | bytes 1048592 | tf_op jit(solution)/shard_map/all_gather | solution.py:72
  71.8 1.4 reduce_sum.60
  73.3 4.3 %gather_fusion.2 = bf16[768,2048]{1,0:T(8,128)(2,1)} fusion(bf16[65,2048]{1,0:T(8,128)(2,1)S(1)} %concatenate.3, s32[1024]{0:T(1024)S(1)} %pad_clamp_fusion.1), kind=kCustom, calls=%fused_computation.2 | custom fusion | bytes 6294528 | tf_op jit(solution)/shard_map/gather | solution.py:100
  77.6 6.1 %reshape.134 = bf16[64,12,2048]{2,1,0:T(8,128)(2,1)} reshape(bf16[768,2048]{1,0:T(8,128)(2,1)} %gather_fusion.2) | data formatting | bytes 6291456 | tf_op jit(solution)/shard_map/reshape | solution.py:100
  83.7 106.9 %all_to_all.29 = bf16[64,12,2048]{2,1,0:T(8,128)(2,1)S(1)} all-to-all(bf16[64,12,2048]{2,1,0:T(8,128)(2,1)} %reshape.134), channel_id=1, replica_groups=mesh['ep'=64,'rep'=4] {'ep'}, dimensions={0} | all-to-all | bytes 6291456 | tf_op jit(solution)/shard_map/all_to_all | solution.py:101
  190.6 2.0 copy-done.2
  192.6 3.1 fusion.9
  195.6 8.8 %convolution_convert_fusion = bf16[64,12,2048]{2,0,1:T(8,128)(2,1)} fusion(bf16[1,352,2048]{2,1,0:T(8,128)(2,1)} %param.33, bf16[1,2048,352]{1,2,0:T(8,128)(2,1)} %param.32, bf16[64,12,2048]{2,1,0:T(8,128)(2,1)} %copy-done.2, f32[64,1,12,352]{3,0,2,1:T(8,128)} %fusion.9), kind=kOutput, calls=%fused_computation.7 | convolution fusion | flops 2217787392 | bytes 10256384 | tf_op jit(solution)/shard_map/secf,efd->secd/dot_general | solution.py:111
  204.4 5.7 %copy.52 = bf16[64,12,2048]{2,1,0:T(8,128)(2,1)} copy(bf16[64,12,2048]{2,0,1:T(8,128)(2,1)} %convolution_convert_fusion) | data formatting | bytes 6291456 | tf_op jit(solution)/shard_map/convert_element_type | solution.py:114
  210.1 5.8 %all-to-all-start.2 = ((bf16[64,12,2048]{2,1,0:T(8,128)(2,1)}), bf16[64,12,2048]{2,1,0:T(8,128)(2,1)}, u32[]{:S(2)}, u32[]{:S(2)}) async-start(bf16[64,12,2048]{2,1,0:T(8,128)(2,1)} %copy.52), calls=%async_computation.2 | async-start | bytes 8388608 | tf_op jit(solution)/shard_map/all_to_all | solution.py:117
  216.2 1.9 fusion.80
  218.2 93.9 %all-to-all-done.2 = bf16[64,12,2048]{2,1,0:T(8,128)(2,1)} async-done(((bf16[64,12,2048]{2,1,0:T(8,128)(2,1)}), bf16[64,12,2048]{2,1,0:T(8,128)(2,1)}, u32[]{:S(2)}, u32[]{:S(2)}) %all-to-all-start.2) | async-done | bytes 3145760 | tf_op jit(solution)/shard_map/all_to_all | solution.py:117
  312.0 6.2 %reshape.139 = bf16[768,2048]{1,0:T(8,128)(2,1)} reshape(bf16[64,12,2048]{2,1,0:T(8,128)(2,1)} %all-to-all-done.2) | data formatting | bytes 6291456 | tf_op jit(solution)/shard_map/reshape | solution.py:118
  318.2 7.4 %gather_fusion.3 = bf16[384,2048]{1,0:T(8,128)(2,1)} fusion(bf16[768,2048]{1,0:T(8,128)(2,1)} %reshape.139, s32[1024]{0:T(1024)S(1)} %pad_clamp_fusion), kind=kCustom, calls=%fused_computation.3 | custom fusion | bytes 3147264 | tf_op jit(solution)/shard_map/gather | solution.py:118
  325.6 3.9 %reshape.140 = f32[64,6,2048]{2,1,0:T(8,128)} reshape(bf16[384,2048]{1,0:T(8,128)(2,1)} %gather_fusion.3) | data formatting | bytes 4718592 | tf_op jit(solution)/shard_map/convert_element_type | solution.py:121
  329.5 3.7 %multiply_reduce_fusion = f32[64,2048]{1,0:T(8,128)S(1)} fusion(f32[64,6,2048]{2,1,0:T(8,128)} %reshape.140, f32[64,6]{1,0:T(8,128)S(1)} %copy.53), kind=kLoop, calls=%fused_computation.6 | loop fusion | flops 1441792 | bytes 3671552 | tf_op jit(solution)/shard_map/reduce_sum | solution.py:120
  333.2 3.7 %fusion.1 = bf16[64,2048]{1,0:T(8,128)(2,1)} fusion(f32[64,2048]{1,0:T(8,128)S(1)} %multiply_reduce_fusion, bf16[352,2048]{1,0:T(8,128)(2,1)} %param.36, bf16[64,2048]{1,0:T(8,128)(2,1)S(1)} %add_convert_fusion, bf16[2048,352]{0,1:T(8,128)(2,1)} %param.35, f32[64,352]{1,0:T(8,128)S(1)} %fusion.80), kind=kOutput, calls=%fused_computation.9 | convolution fusion | flops 184946688 | bytes 4022272 | tf_op jit(solution)/shard_map/dot_general | solution.py:79
  337.0 18.5 %reduce-scatter.2.cloned.1.call-done = bf16[16,2048]{1,0:T(8,128)(2,1)} async-done(((bf16[64,2048]{1,0:T(8,128)(2,1)}), bf16[16,2048]{1,0:T(8,128)(2,1)}) %reduce-scatter.2.cloned.1.call-update) | async-done | bytes 65552 | tf_op jit(solution)/shard_map/reduce_scatter | solution.py:126
  355.4 1.0 multiply_reduce_fusion.1
  356.4 1.6 multiply_convert_fusion
  (57 shorter events, 3.9 us)
Async XLA Ops:
  6.5 36.4 %copy-start = (bf16[512,2048]{1,0:T(8,128)(2,1)S(1)}, bf16[512,2048]{1,0:T(8,128)(2,1)}, u32[]{:S(2)}) copy-start(bf16[512,2048]{1,0:T(8,128)(2,1)} %param.27) | copy-start | bytes 6291460
  6.5 65.3 %all-gather.3.cloned.1.call-start = ((), (), s32[]{:S(2)}) async-start(), calls=%async_computation.5 | async-start | bytes 1310720 | tf_op jit(solution)/shard_map/all_gather | solution.py:72
  8.5 8.8 %copy-start.1 = (bf16[32,2048]{1,0:T(8,128)(2,1)S(1)}, bf16[32,2048]{1,0:T(8,128)(2,1)}, u32[]{:S(2)}) copy-start(bf16[32,2048]{1,0:T(8,128)(2,1)} %param.23) | copy-start | bytes 393220
  19.2 3.7 %copy-start.11 = (s32[16]{0:T(128)S(1)}, s32[16]{0:T(128)}, u32[]{:S(2)}) copy-start(s32[16]{0:T(128)} %param.25) | copy-start | bytes 196
  23.0 3.7 %copy-start.6 = (bf16[16,16,64]{2,1,0:T(8,128)(2,1)S(1)}, bf16[16,16,64]{2,1,0:T(8,128)(2,1)}, u32[]{:S(2)}) copy-start(bf16[16,16,64]{2,1,0:T(8,128)(2,1)} %reshape.131) | copy-start | bytes 98308
  27.1 0.8 copy-start.3
  31.7 11.0 %copy-start.4 = (bf16[4,512,128]{2,1,0:T(8,128)(2,1)S(1)}, bf16[4,512,128]{2,1,0:T(8,128)(2,1)}, u32[]{:S(2)}) copy-start(bf16[4,512,128]{2,1,0:T(8,128)(2,1)} %param.26) | copy-start | bytes 1572868
  42.7 1.5 copy-start.9
  42.7 1.5 copy-start.10
  44.1 29.1 %copy-start.5 = (bf16[64,2048]{1,0:T(8,128)(2,1)S(1)}, bf16[64,2048]{1,0:T(8,128)(2,1)}, u32[]{:S(2)}) copy-start(bf16[64,2048]{1,0:T(8,128)(2,1)} %param.19) | copy-start | bytes 786436
  83.7 108.9 %copy-start.12 = (bf16[1,2048,352]{1,2,0:T(8,128)(2,1)S(1)}, bf16[1,2048,352]{1,2,0:T(8,128)(2,1)}, u32[]{:S(2)}) copy-start(bf16[1,2048,352]{1,2,0:T(8,128)(2,1)} %param.31) | copy-start | bytes 4325380
  190.6 2.0 copy-start.2
  210.1 6.0 %copy-start.8 = (f32[64,6]{0,1:T(8,128)S(1)}, f32[64,6]{0,1:T(8,128)}, u32[]{:S(2)}) copy-start(f32[64,6]{0,1:T(8,128)} %param.29) | copy-start | bytes 4612
  210.1 101.9 %all-to-all-start.2 = ((bf16[64,12,2048]{2,1,0:T(8,128)(2,1)}), bf16[64,12,2048]{2,1,0:T(8,128)(2,1)}, u32[]{:S(2)}, u32[]{:S(2)}) async-start(bf16[64,12,2048]{2,1,0:T(8,128)(2,1)} %copy.52), calls=%async_computation.2 | async-start | bytes 8388608 | tf_op jit(solution)/shard_map/all_to_all | solution.py:117
  215.9 139.6 %reduce-scatter.2.cloned.1.call-start = ((), (), s32[]{:S(2)}) async-start(), calls=%async_computation.4 | async-start | bytes 327680 | tf_op jit(solution)/shard_map/reduce_scatter | solution.py:126
  333.2 23.2 %copy-start.7 = (f32[2048]{0:T(1024)S(1)}, f32[2048]{0:T(1024)}, u32[]{:S(2)}) copy-start(f32[2048]{0:T(1024)} %param.37) | copy-start | bytes 24580
Sparse Core Ops, SparseCore 0:
  44.3 27.4 all-gather.2
  337.1 18.3 reduce-scatter.1
